TPU v7x, 512 devices: a whole 4x8x8 slice. The times are simulated.
512 devices in a mesh: seq: 128 (over y, z, core), tp: 4 (over x).
Axes of the slice: x: 4, y: 8, z: 8, core: 2. Of those that a mesh axis runs over, the one named last changes fastest.
Arguments:
- queries: bfloat16 [16384, 4096], P('seq', 'tp'), may hold values from -12 to 12
- keys: bfloat16 [16384, 512], P('seq', 'tp'), may hold values from -12 to 12
- values: bfloat16 [16384, 512], P('seq', 'tp'), may hold values from -6 to 6
- sinks: float32 [64], P('tp'), may hold values from 0.5 to 4.5
- session_start: int32 [16384], P('seq'), may hold values from 0 to 16383, as said below
- residual: bfloat16 [16384, 2880], P('seq', 'tp'), may hold values from -40 to 40
- w_out: bfloat16 [4096, 2880], P('seq', 'tp'), may hold values from -0.09375 to 0.09375
- norm_gain: float32 [2880], P('tp'), may hold values from 0.1 to 1.9
- expert_ids: int32 [16384, 4], P('seq'), may hold values from 0 to 63, all different within a row; in each aligned block of 128 rows (0 to 127, 128 to 255, ...) at most 10 rows name the same one
- expert_gates: bfloat16 [16384, 4], P('seq'), may hold values from 0.099609375 to 0.59765625
- w_gate: bfloat16 [2880, 92160], P('tp', 'seq'), may hold values from -0.109375 to 0.109375
- w_up: bfloat16 [2880, 92160], P('tp', 'seq'), may hold values from -0.109375 to 0.109375
- w_down: bfloat16 [92160, 2880], P('seq', 'tp'), may hold values from -0.15625 to 0.15625
Outputs:
- layer_out: bfloat16 [16384, 2880], P('seq', 'tp')
Inputs may be any that keep to these rules, and one draw needn't show every extreme that they name: `expert_ids`: each row names 4 different experts. Within the rows of one seq index (aligned blocks of 128 rows) no expert is named by more than 10 rows, a bound that some block reaches. `session_start`: nondecreasing; each entry is the first position of its token's session, so session_start[i] <= i, with equality at a session's first token.
All inputs are finite; a program needn't handle non-finite values.
Results may differ from a plain program's by a relative error of at most 0.013.
Values may be sent and summed in bfloat16 or wider, within the bound.
No kernel may reach another device: no remote copies, remote signals or barrier semaphores. Data moves between devices by JAX's collectives and lax.ppermute only.
A program may use at most 64 MiB of HBM per device.

v0:
```python
import jax
import jax.numpy as jnp
from jax import lax
from jax.sharding import PartitionSpec as P

D = 2880
HEAD_SIZE = 64
WINDOW_SPAN = 128
TOP = 4
NEGATIVE = -1e30
EPSILON = 1e-05


def passed_along(block, axis, distance):
    devices = range(lax.axis_size(axis))
    route = [(i - distance, i) for i in devices if i - distance in devices]
    return lax.ppermute(block, axis, route)


def shards(
    queries,
    keys,
    values,
    sinks,
    session_start,
    residual,
    w_out,
    norm_gain,
    expert_ids,
    expert_gates,
    w_gate,
    w_up,
    w_down,
):
    tok_count = queries.shape[0]
    kv_heads = keys.shape[1] // HEAD_SIZE
    q_heads = queries.shape[1] // HEAD_SIZE
    query_groups = q_heads // kv_heads
    seq_index = lax.axis_index("seq")
    first_pos = seq_index * tok_count
    tail_rows = passed_along((keys, values), "seq", 1)
    all_keys = jnp.concatenate([tail_rows[0], keys], axis=0)
    all_values = jnp.concatenate([tail_rows[1], values], axis=0)
    key_count = all_keys.shape[0]
    query_pos = first_pos + jnp.arange(tok_count, dtype=jnp.int32)
    key_pos = first_pos - WINDOW_SPAN + jnp.arange(key_count, dtype=jnp.int32)
    distance = query_pos[:, None] - key_pos[None, :]
    allowed = (
        (distance >= 0) & (distance < WINDOW_SPAN) & (key_pos[None, :] >= session_start[:, None])
    )
    blocked_queries = queries.reshape(tok_count, kv_heads, query_groups, HEAD_SIZE)
    blocked_keys = all_keys.reshape(key_count, kv_heads, HEAD_SIZE)
    blocked_values = all_values.reshape(key_count, kv_heads, HEAD_SIZE)
    scores = jnp.einsum(
        "qhgd,khd->hgqk", blocked_queries, blocked_keys, preferred_element_type=jnp.float32
    ) * HEAD_SIZE ** (-0.5)
    scores = jnp.where(allowed[None, None], scores, NEGATIVE)
    sink_column = sinks.reshape(kv_heads, query_groups)[:, :, None, None]
    row_max = jnp.maximum(jnp.max(scores, axis=-1, keepdims=True), sink_column)
    numerator = jnp.exp(scores - row_max) * allowed[None, None].astype(jnp.float32)
    denominator = jnp.sum(numerator, axis=-1, keepdims=True) + jnp.exp(sink_column - row_max)
    weights = (numerator / denominator).astype(jnp.bfloat16)
    head_out = jnp.einsum(
        "hgqk,khd->qhgd", weights, blocked_values, preferred_element_type=jnp.float32
    )
    head_out = head_out.astype(jnp.bfloat16).reshape(tok_count, q_heads * HEAD_SIZE)
    gathered = lax.all_gather(head_out, "tp", axis=1, tiled=True)
    attended = jnp.dot(
        gathered,
        lax.all_gather(w_out, "seq", axis=0, tiled=True),
        preferred_element_type=jnp.float32,
    )
    stream = residual.astype(jnp.float32) + attended
    squares = lax.psum(jnp.sum(stream * stream, axis=1), "tp")
    normed = (stream * lax.rsqrt(squares / D + EPSILON)[:, None] * norm_gain[None, :]).astype(
        jnp.bfloat16
    )
    seq_count = lax.axis_size("seq")
    experts = seq_count // 2
    capacity = 2 * ((5 * tok_count * TOP + 8 * experts - 1) // (8 * experts))
    present = expert_ids[:, :, None] == jnp.arange(experts, dtype=jnp.int32)[None, None, :]
    per_row = jnp.sum(present.astype(jnp.int32), axis=1)
    before = jnp.cumsum(per_row, axis=0) - per_row
    position = jnp.sum(jnp.where(present, before[:, None, :], 0), axis=2)
    halves = jnp.arange(2, dtype=jnp.int32)
    targets = (2 * expert_ids[:, :, None] + halves[None, None, :]) * capacity + position[:, :, None]
    slot_count = seq_count * capacity
    slot_ids = jnp.arange(slot_count, dtype=jnp.int32)
    quarter = normed.shape[1]
    matches = (slot_ids[:, None, None, None] == targets[None]).astype(jnp.bfloat16)
    routing = jnp.sum(matches, axis=(2, 3))
    sending = jnp.dot(routing, normed, preferred_element_type=jnp.float32).astype(jnp.bfloat16)
    arrived = lax.all_to_all(
        sending.reshape(seq_count, capacity, quarter),
        "seq",
        split_axis=0,
        concat_axis=0,
        tiled=True,
    )
    expert_rows = arrived.reshape(slot_count, quarter)
    gate_part = jnp.dot(expert_rows, w_gate, preferred_element_type=jnp.float32)
    up_part = jnp.dot(expert_rows, w_up, preferred_element_type=jnp.float32)
    gate_sum, up_sum = (
        lax.psum_scatter(
            gate_part.astype(jnp.bfloat16), "tp", scatter_dimension=1, tiled=True
        ).astype(jnp.float32),
        lax.psum_scatter(
            up_part.astype(jnp.bfloat16), "tp", scatter_dimension=1, tiled=True
        ).astype(jnp.float32),
    )
    active = (jax.nn.silu(gate_sum) * up_sum).astype(jnp.bfloat16)
    produced = jnp.dot(
        lax.all_gather(active, "tp", axis=1, tiled=True), w_down, preferred_element_type=jnp.float32
    )
    produced = produced.astype(jnp.bfloat16).reshape(seq_count, capacity, quarter)
    returned = lax.all_to_all(produced, "seq", split_axis=0, concat_axis=0, tiled=True)
    both = returned.reshape(experts, 2, capacity, quarter)
    paired = (both[:, 0].astype(jnp.float32) + both[:, 1].astype(jnp.float32)).astype(jnp.bfloat16)
    paired = paired.reshape(experts * capacity, quarter)
    pair_slot = expert_ids * capacity + position
    pair_ids = jnp.arange(experts * capacity, dtype=jnp.int32)
    mixing = jnp.where(
        pair_ids[None, :, None] == pair_slot[:, None, :],
        expert_gates[:, None, :],
        jnp.zeros((), jnp.bfloat16),
    )
    mixing = jnp.sum(mixing, axis=2)
    blended = jnp.dot(mixing, paired, preferred_element_type=jnp.float32)
    return (stream + blended).astype(jnp.bfloat16)


def solution(mesh):
    return jax.shard_map(
        shards,
        mesh=mesh,
        in_specs=(
            P("seq", "tp"),
            P("seq", "tp"),
            P("seq", "tp"),
            P("tp"),
            P("seq"),
            P("seq", "tp"),
            P("seq", "tp"),
            P("tp"),
            P("seq", None),
            P("seq", None),
            P("tp", "seq"),
            P("tp", "seq"),
            P("seq", "tp"),
        ),
        out_specs=P("seq", "tp"),
        check_vma=False,
    )
```

profile of v0, /device:TPU:72, one launch (start us, length us, event | category | flops | bytes accessed | tf_op | source)
XLA Modules:
  0.0 459.0 jit_solution(16349413189414434142)
XLA Ops:
  6.5 2.0 collective-permute-start.1
  8.6 4.4 collective-permute-start
  23.4 30.5 %all-gather.5.cloned.1.call-done = bf16[128,4096]{0,1:T(8,128)(2,1)} async-done(((bf16[128,1024]{0,1:T(8,128)(2,1)}), bf16[128,4096]{0,1:T(8,128)(2,1)}) %all-gather.5.cloned.1.call-update) | async-done | bytes 1048592 | tf_op jit(solution)/shard_map/all_gather | solution.py:67
  53.9 88.6 %all-gather.7.cloned.1.call-done = bf16[4096,720]{1,0:T(8,128)(2,1)} async-done(((bf16[32,720]{1,0:T(8,128)(2,1)}), bf16[4096,720]{1,0:T(8,128)(2,1)}) %all-gather.7.cloned.1.call-update) | async-done | bytes 5898256 | tf_op jit(solution)/shard_map/all_gather | solution.py:70
  142.5 5.1 %multiply_reduce_fusion = (f32[128]{0:T(128)S(1)}, f32[128,720]{0,1:T(8,128)S(1)}) fusion(bf16[128,4096]{0,1:T(8,128)(2,1)} %all-gather.5.cloned.1.call-done, bf16[4096,720]{1,0:T(8,128)(2,1)} %all-gather.7.cloned.1.call-done, bf16[128,720]{0,1:T(8,128)(2,1)} %param.18), kind=kOutput, calls=%fused_computation.31 | convolution fusion | flops 755343232 | bytes 7500288 | tf_op jit(solution)/shard_map/dot_general | solution.py:68
  147.6 10.4 %psum.7 = f32[128]{0:T(128)S(1)} all-reduce(f32[128]{0:T(128)S(1)} %get-tuple-element.15), channel_id=1, replica_groups=mesh['seq'=128,'tp'=4] {'tp'}, use_global_device_ids=true, to_apply=%region_8.9 | all-reduce | flops 128 | bytes 1024 | tf_op jit(solution)/shard_map/psum | solution.py:74
  158.0 2.0 convolution_convert_fusion
  160.0 2.6 copy.56
  162.6 2.5 reshape.190
  165.1 86.3 %all_to_all.10 = bf16[128,10,720]{2,1,0:T(8,128)(2,1)} all-to-all(bf16[128,10,720]{2,1,0:T(8,128)(2,1)} %reshape.190), channel_id=1, replica_groups=mesh['seq'=128,'tp'=4] {'seq'}, dimensions={0} | all-to-all | bytes 3686400 | tf_op jit(solution)/shard_map/all_to_all | solution.py:93
  251.4 3.9 reshape.191
  255.4 3.0 convolution_convert_fusion.2
  258.4 2.9 convolution_convert_fusion.3
  261.3 46.3 %fusion.22 = (bf16[1280,184]{0,1:T(8,128)(2,1)S(1)}, bf16[1280,184]{0,1:T(8,128)(2,1)S(1)}) fusion(bf16[1280,720]{0,1:T(8,128)(2,1)} %convolution_convert_fusion.2, bf16[1280,720]{0,1:T(8,128)(2,1)} %convolution_convert_fusion.3), kind=kCustom, calls=%all-reduce-scatter.2 | all-reduce-scatter fusion | flops 1884161 | bytes 4630528
  309.0 3.3 collective-permute-start.3
  316.8 29.1 %all-gather.9.cloned.1.call-done = bf16[4,180,1280]{2,1,0:T(8,128)(2,1)} async-done(((bf16[1,180,1280]{2,1,0:T(8,128)(2,1)}), bf16[4,180,1280]{2,1,0:T(8,128)(2,1)}) %all-gather.9.cloned.1.call-update) | async-done | bytes 1843216 | tf_op jit(solution)/shard_map/all_gather | solution.py:113
  345.9 1.7 reshape.195
  347.5 4.2 convolution_convert_fusion.1
  351.8 2.6 copy.57
  354.4 2.5 reshape.192
  356.9 14.5 %all-to-all-start.1 = ((bf16[128,10,720]{2,1,0:T(8,128)(2,1)}), bf16[128,10,720]{2,1,0:T(8,128)(2,1)}, u32[]{:S(2)}, u32[]{:S(2)}) async-start(bf16[128,10,720]{2,1,0:T(8,128)(2,1)} %reshape.192), calls=%async_computation.1 | async-start | bytes 6291456 | tf_op jit(solution)/shard_map/all_to_all | solution.py:116
  371.7 74.7 %all-to-all-done.1 = bf16[128,10,720]{2,1,0:T(8,128)(2,1)} async-done(((bf16[128,10,720]{2,1,0:T(8,128)(2,1)}), bf16[128,10,720]{2,1,0:T(8,128)(2,1)}, u32[]{:S(2)}, u32[]{:S(2)}) %all-to-all-start.1) | async-done | bytes 1843232 | tf_op jit(solution)/shard_map/all_to_all | solution.py:116
  446.4 2.3 add_convert_fusion
  450.1 2.4 fusion.7
  (59 shorter events, 17.0 us)
Async XLA Ops:
  6.5 248.8 %copy-start = (bf16[720,720]{1,0:T(8,128)(2,1)S(1)}, bf16[720,720]{1,0:T(8,128)(2,1)}, u32[]{:S(2)}) copy-start(bf16[720,720]{1,0:T(8,128)(2,1)} %param.24) | copy-start | bytes 3110404
  6.5 47.4 %all-gather.5.cloned.1.call-start = ((), (), s32[]{:S(2)}) async-start(), calls=%async_computation.2 | async-start | bytes 1310720 | tf_op jit(solution)/shard_map/all_gather | solution.py:67
  6.5 9.8 %collective-permute-start.1 = (bf16[128,128]{1,0:T(8,128)(2,1)}, bf16[128,128]{1,0:T(8,128)(2,1)S(1)}, u32[]{:S(2)}, u32[]{:S(2)}) collective-permute-start(bf16[128,128]{1,0:T(8,128)(2,1)} %param.14), channel_id=1, source_target_pairs={{0,4},{4,8},{8,12},{12,16},{16,20},{20,24},{24,28},{28,32},{32,36}... | collective-permute-start | bytes 98312 | tf_op jit(solution)/shard_map/ppermute | solution.py:17
  8.6 11.3 %collective-permute-start = (bf16[128,128]{1,0:T(8,128)(2,1)}, bf16[128,128]{1,0:T(8,128)(2,1)S(1)}, u32[]{:S(2)}, u32[]{:S(2)}) collective-permute-start(bf16[128,128]{1,0:T(8,128)(2,1)} %param.15), channel_id=1, source_target_pairs={{0,4},{4,8},{8,12},{12,16},{16,20},{20,24},{24,28},{28,32},{32,36}... | collective-permute-start | bytes 98312 | tf_op jit(solution)/shard_map/ppermute | solution.py:17
  17.8 1.5 copy-start.1
  17.8 2.0 copy-start.3
  19.2 0.9 copy-start.2
  20.1 2.2 copy-start.4
  21.5 121.0 %all-gather.7.cloned.1.call-start = ((), (), s32[]{:S(2)}) async-start(), calls=%async_computation.3 | async-start | bytes 6340608 | tf_op jit(solution)/shard_map/all_gather | solution.py:70
  22.3 323.6 %all-gather.9.cloned.1.call-start = ((), (), s32[]{:S(2)}) async-start(), calls=%async_computation.4 | async-start | bytes 2355200 | tf_op jit(solution)/shard_map/all_gather | solution.py:113
  23.4 134.6 %copy-start.5 = (f32[720]{0:T(1024)S(1)}, f32[720]{0:T(1024)}, u32[]{:S(2)}) copy-start(f32[720]{0:T(1024)} %param.20) | copy-start | bytes 8644
  255.4 3.0 copy-start.7
  307.7 6.6 %collective-permute-start.2 = (bf16[1280,12]{0,1:T(8,128)(2,1)S(1)}, bf16[1280,12]{0,1:T(8,128)(2,1)S(1)}, u32[]{:S(2)}, u32[]{:S(2)}) collective-permute-start(bf16[1280,12]{0,1:T(8,128)(2,1)S(1)} %slice.10), channel_id=1, source_target_pairs={{0,1},{1,2},{2,3},{4,5},{5,6},{6,7},{8,9},{9,10},{10,11},{12,13},{... | collective-permute-start | bytes 92168
  309.0 5.9 %collective-permute-start.3 = (bf16[1280,12]{0,1:T(8,128)(2,1)S(1)}, bf16[1280,12]{0,1:T(8,128)(2,1)S(1)}, u32[]{:S(2)}, u32[]{:S(2)}) collective-permute-start(bf16[1280,12]{0,1:T(8,128)(2,1)S(1)} %slice.11), channel_id=1, source_target_pairs={{0,1},{1,2},{2,3},{4,5},{5,6},{6,7},{8,9},{9,10},{10,11},{12,13},{... | collective-permute-start | bytes 92168
  356.9 14.5 %copy-start.6 = (bf16[128,4]{0,1:T(4,128)(2,1)S(1)}, bf16[128,4]{0,1:T(4,128)(2,1)}, u32[]{:S(2)}) copy-start(bf16[128,4]{0,1:T(4,128)(2,1)} %param.22) | copy-start | bytes 3076
  356.9 89.5 %all-to-all-start.1 = ((bf16[128,10,720]{2,1,0:T(8,128)(2,1)}), bf16[128,10,720]{2,1,0:T(8,128)(2,1)}, u32[]{:S(2)}, u32[]{:S(2)}) async-start(bf16[128,10,720]{2,1,0:T(8,128)(2,1)} %reshape.192), calls=%async_computation.1 | async-start | bytes 6291456 | tf_op jit(solution)/shard_map/all_to_all | solution.py:116
Sparse Core Ops, SparseCore 0:
  21.6 32.2 all-gather.4
  57.0 85.4 all-gather.6
  316.9 28.9 all-gather.8
where the time goes:
time: 460 us; the launch traced here: 459 us
  waiting for transfers between devices  224 us (49%)
  blocking collectives  143 us (31%)
  starting transfers between devices  25.6 us (6%)
  local copies, waits for them, and re-layouts  22.8 us (5%)
  matrix products  22.4 us (5%)
  between operations  14.1 us (3%)
  other arithmetic  7.47 us (2%)
    all_gather x1, waiting for transfers between devices, shards(): lax.all_gather(w_out, 'seq', axis=0, tiled=True)  88.6 us
    all_to_all x1, blocking collectives, shards(): lax.all_to_all(sending.reshape(seq_count, capacity, quarter), 'seq', spli...  86.3 us
    all_to_all x1, waiting for transfers between devices, shards(): lax.all_to_all(produced, 'seq', split_axis=0, concat_axis=0, tiled=True)  74.7 us
    unnamed x1, blocking collectives  46.3 us
    all_gather x1, waiting for transfers between devices, shards(): gathered = lax.all_gather(head_out, 'tp', axis=1, tiled=True)  30.5 us
    all_gather x1, waiting for transfers between devices, shards(): lax.all_gather(active, 'tp', axis=1, tiled=True)  29.1 us
    all_to_all x1, starting transfers between devices, shards(): lax.all_to_all(produced, 'seq', split_axis=0, concat_axis=0, tiled=True)  14.5 us
    psum x1, blocking collectives, shards(): squares = lax.psum(jnp.sum(stream * stream, axis=1), 'tp')  10.4 us
  transfers between devices with their start and end apart: 8, of which 4 were waited for; matrix products, arithmetic and copies ran while one was open for 2% of the time, Pallas kernels for 0%

commit v1 on v0

--- a/solution.py
+++ b/solution.py
@@ -64,7 +64,12 @@
         "hgqk,khd->qhgd", weights, blocked_values, preferred_element_type=jnp.float32
     )
     head_out = head_out.astype(jnp.bfloat16).reshape(tok_count, q_heads * HEAD_SIZE)
-    gathered = lax.all_gather(head_out, "tp", axis=1, tiled=True)
+    ring = [head_out]
+    for hop in range(3):
+        ring.append(lax.ppermute(ring[-1], "tp", [(dev, (dev + 1) % 4) for dev in range(4)]))
+    gathered = jnp.roll(
+        jnp.concatenate(ring[::-1], axis=1), (lax.axis_index("tp") + 1) * ring[0].shape[1], axis=1
+    )
     attended = jnp.dot(
         gathered,
         lax.all_gather(w_out, "seq", axis=0, tiled=True),

time: 460 us -> 417 us (0.907)
  waiting for transfers between devices: 224 us -> 170 us
  starting transfers between devices: 25.6 us -> 32.9 us
  local copies, waits for them, and re-layouts: 22.8 us -> 27.8 us
    all_gather x1, waiting for transfers between devices: 88.6 us -> 42.3 us  [shards(): lax.all_gather(w_out, 'seq', axis=0, tiled=True)]
    all_gather x1 -> x0, waiting for transfers between devices: 30.5 us -> none  [shards(): gathered = lax.all_gather(head_out, 'tp', axis=1, tiled=True)]
    ppermute x0 -> x3, waiting for transfers between devices: none -> 22.7 us  [shards(): lax.ppermute(ring[-1], 'tp', [(dev, (dev + 1) % 4) for dev in range(4)])]
    ppermute x0 -> x3, starting transfers between devices: none -> 7.48 us  [shards(): lax.ppermute(ring[-1], 'tp', [(dev, (dev + 1) % 4) for dev in range(4)])]
    unnamed x23 -> x26, local copies, waits for them, and re-layouts: 5.47 us -> 10.4 us
  transfers between devices with their start and end apart: 8 -> 10, of which waited for: 4 -> 6; matrix products, arithmetic and copies ran while one was open for 2% -> 4% of each run, Pallas kernels for 0% -> 0%
where the time goes in v1:
time: 417 us; the launch traced here: 416 us
  waiting for transfers between devices  170 us (41%)
  blocking collectives  143 us (34%)
  starting transfers between devices  32.9 us (8%)
  local copies, waits for them, and re-layouts  27.8 us (7%)
  matrix products  20.9 us (5%)
  between operations  14.4 us (3%)
  other arithmetic  7.56 us (2%)
    all_to_all x1, blocking collectives, shards(): lax.all_to_all(sending.reshape(seq_count, capacity, quarter), 'seq', spli...  86.3 us
    all_to_all x1, waiting for transfers between devices, shards(): lax.all_to_all(produced, 'seq', split_axis=0, concat_axis=0, tiled=True)  74.7 us
    unnamed x1, blocking collectives  46.3 us
    all_gather x1, waiting for transfers between devices, shards(): lax.all_gather(w_out, 'seq', axis=0, tiled=True)  42.3 us
    all_gather x1, waiting for transfers between devices, shards(): lax.all_gather(active, 'tp', axis=1, tiled=True)  29.1 us
    ppermute x3, waiting for transfers between devices, shards(): lax.ppermute(ring[-1], 'tp', [(dev, (dev + 1) % 4) for dev in range(4)])  22.7 us
    all_to_all x1, starting transfers between devices, shards(): lax.all_to_all(produced, 'seq', split_axis=0, concat_axis=0, tiled=True)  14.5 us
    unnamed x26, local copies, waits for them, and re-layouts  10.4 us
  transfers between devices with their start and end apart: 10, of which 6 were waited for; matrix products, arithmetic and copies ran while one was open for 4% of the time, Pallas kernels for 0%

profile of v1, /device:TPU:72, one launch (start us, length us, event | category | flops | bytes accessed | tf_op | source)
XLA Modules:
  0.0 416.3 jit_solution(6435515076640871028)
XLA Ops:
  9.2 4.4 %collective-permute-start = (bf16[128,128]{1,0:T(8,128)(2,1)}, bf16[128,128]{1,0:T(8,128)(2,1)S(1)}, u32[]{:S(2)}, u32[]{:S(2)}) collective-permute-start(bf16[128,128]{1,0:T(8,128)(2,1)} %param.15), channel_id=1, source_target_pairs={{0,4},{4,8},{8,12},{12,16},{16,20},{20,24},{24,28},{28,32},{32,36}... | collective-permute-start | bytes 98312 | tf_op jit(solution)/shard_map/ppermute | solution.py:17
  19.9 3.4 collective-permute-start.2
  23.7 7.5 %collective-permute-done.2 = bf16[128,1024]{0,1:T(8,128)(2,1)S(1)} collective-permute-done((bf16[128,1024]{0,1:T(8,128)(2,1)S(1)}, bf16[128,1024]{0,1:T(8,128)(2,1)S(1)}, u32[]{:S(2)}, u32[]{:S(2)}) %collective-permute-start.2) | collective-permute-done | bytes 262176 | tf_op jit(solution)/shard_map/ppermute | solution.py:69
  33.5 8.2 %collective-permute-done.3 = bf16[128,1024]{0,1:T(8,128)(2,1)S(1)} collective-permute-done((bf16[128,1024]{0,1:T(8,128)(2,1)S(1)}, bf16[128,1024]{0,1:T(8,128)(2,1)S(1)}, u32[]{:S(2)}, u32[]{:S(2)}) %collective-permute-start.3) | collective-permute-done | bytes 262176 | tf_op jit(solution)/shard_map/ppermute | solution.py:69
  44.4 6.9 %collective-permute-done.4 = bf16[128,1024]{0,1:T(8,128)(2,1)S(1)} collective-permute-done((bf16[128,1024]{0,1:T(8,128)(2,1)S(1)}, bf16[128,1024]{0,1:T(8,128)(2,1)S(1)}, u32[]{:S(2)}, u32[]{:S(2)}) %collective-permute-start.4) | collective-permute-done | bytes 262176 | tf_op jit(solution)/shard_map/ppermute | solution.py:69
  57.1 42.3 %all-gather.4.cloned.1.call-done = bf16[4096,720]{1,0:T(8,128)(2,1)} async-done(((bf16[32,720]{1,0:T(8,128)(2,1)}), bf16[4096,720]{1,0:T(8,128)(2,1)}) %all-gather.4.cloned.1.call-update) | async-done | bytes 5898256 | tf_op jit(solution)/shard_map/all_gather | solution.py:75
  99.4 5.2 %multiply_reduce_fusion = (f32[128]{0:T(128)S(1)}, f32[128,720]{0,1:T(8,128)S(1)}) fusion(bf16[4096,720]{1,0:T(8,128)(2,1)} %all-gather.4.cloned.1.call-done, bf16[128,8192]{0,1:T(8,128)(2,1)} %constant_dynamic-update-slice_fusion, s32[]{:T(128)S(6)} %select_n.27, bf16[128,720]{0,1:T(8,128)(2,1)S(1)} %copy-done.1), kind=kOutput, calls=%fused_computation.32 | convolution fusion | flops 755343232 | bytes 7893508 | tf_op jit(solution)/shard_map/dot_general | solution.py:73
  104.6 10.4 %psum.7 = f32[128]{0:T(128)S(1)} all-reduce(f32[128]{0:T(128)S(1)} %get-tuple-element.15), channel_id=1, replica_groups=mesh['seq'=128,'tp'=4] {'tp'}, use_global_device_ids=true, to_apply=%region_8.9 | all-reduce | flops 128 | bytes 1024 | tf_op jit(solution)/shard_map/psum | solution.py:79
  117.0 2.6 copy.56
  119.7 2.5 reshape.190
  122.1 86.3 %all_to_all.10 = bf16[128,10,720]{2,1,0:T(8,128)(2,1)} all-to-all(bf16[128,10,720]{2,1,0:T(8,128)(2,1)} %reshape.190), channel_id=1, replica_groups=mesh['seq'=128,'tp'=4] {'seq'}, dimensions={0} | all-to-all | bytes 3686400 | tf_op jit(solution)/shard_map/all_to_all | solution.py:98
  208.4 3.9 reshape.191
  212.4 3.0 convolution_convert_fusion.2
  215.4 2.9 convolution_convert_fusion.3
  218.3 46.3 %fusion.24 = (bf16[1280,184]{0,1:T(8,128)(2,1)S(1)}, bf16[1280,184]{0,1:T(8,128)(2,1)S(1)}) fusion(bf16[1280,720]{0,1:T(8,128)(2,1)} %convolution_convert_fusion.2, bf16[1280,720]{0,1:T(8,128)(2,1)} %convolution_convert_fusion.3), kind=kCustom, calls=%all-reduce-scatter.2 | all-reduce-scatter fusion | flops 1884161 | bytes 4630528
  266.0 3.3 collective-permute-start.6
  273.8 29.1 %all-gather.6.cloned.1.call-done = bf16[4,180,1280]{2,1,0:T(8,128)(2,1)} async-done(((bf16[1,180,1280]{2,1,0:T(8,128)(2,1)}), bf16[4,180,1280]{2,1,0:T(8,128)(2,1)}) %all-gather.6.cloned.1.call-update) | async-done | bytes 1843216 | tf_op jit(solution)/shard_map/all_gather | solution.py:118
  304.6 4.2 %convolution_convert_fusion.1 = bf16[1280,720]{0,1:T(8,128)(2,1)} fusion(bf16[720,1280]{1,0:T(8,128)(2,1)S(1)} %reshape.195, bf16[720,720]{1,0:T(8,128)(2,1)} %param.25), kind=kOutput, calls=%fused_computation.3 | convolution fusion | flops 1328025600 | bytes 4723200 | tf_op jit(solution)/shard_map/dot_general | solution.py:117
  308.8 2.6 copy.57
  311.4 2.5 reshape.192
  313.9 14.5 %all-to-all-start.1 = ((bf16[128,10,720]{2,1,0:T(8,128)(2,1)}), bf16[128,10,720]{2,1,0:T(8,128)(2,1)}, u32[]{:S(2)}, u32[]{:S(2)}) async-start(bf16[128,10,720]{2,1,0:T(8,128)(2,1)} %reshape.192), calls=%async_computation.1 | async-start | bytes 6291456 | tf_op jit(solution)/shard_map/all_to_all | solution.py:121
  328.7 74.7 %all-to-all-done.1 = bf16[128,10,720]{2,1,0:T(8,128)(2,1)} async-done(((bf16[128,10,720]{2,1,0:T(8,128)(2,1)}), bf16[128,10,720]{2,1,0:T(8,128)(2,1)}, u32[]{:S(2)}, u32[]{:S(2)}) %all-to-all-start.1) | async-done | bytes 1843232 | tf_op jit(solution)/shard_map/all_to_all | solution.py:121
  403.4 2.3 add_convert_fusion
  407.1 2.4 fusion.7
  (66 shorter events, 30.2 us)
Async XLA Ops:
  6.5 205.8 %copy-start = (bf16[720,720]{1,0:T(8,128)(2,1)S(1)}, bf16[720,720]{1,0:T(8,128)(2,1)}, u32[]{:S(2)}) copy-start(bf16[720,720]{1,0:T(8,128)(2,1)} %param.24) | copy-start | bytes 3110404
  6.5 92.9 %all-gather.4.cloned.1.call-start = ((), (), s32[]{:S(2)}) async-start(), calls=%async_computation.2 | async-start | bytes 6340608 | tf_op jit(solution)/shard_map/all_gather | solution.py:75
  7.3 295.6 %all-gather.6.cloned.1.call-start = ((), (), s32[]{:S(2)}) async-start(), calls=%async_computation.3 | async-start | bytes 2355200 | tf_op jit(solution)/shard_map/all_gather | solution.py:118
  7.3 9.0 %collective-permute-start.1 = (bf16[128,128]{1,0:T(8,128)(2,1)}, bf16[128,128]{1,0:T(8,128)(2,1)S(1)}, u32[]{:S(2)}, u32[]{:S(2)}) collective-permute-start(bf16[128,128]{1,0:T(8,128)(2,1)} %param.14), channel_id=1, source_target_pairs={{0,4},{4,8},{8,12},{12,16},{16,20},{20,24},{24,28},{28,32},{32,36}... | collective-permute-start | bytes 98312 | tf_op jit(solution)/shard_map/ppermute | solution.py:17
  9.2 7.9 %collective-permute-start = (bf16[128,128]{1,0:T(8,128)(2,1)}, bf16[128,128]{1,0:T(8,128)(2,1)S(1)}, u32[]{:S(2)}, u32[]{:S(2)}) collective-permute-start(bf16[128,128]{1,0:T(8,128)(2,1)} %param.15), channel_id=1, source_target_pairs={{0,4},{4,8},{8,12},{12,16},{16,20},{20,24},{24,28},{28,32},{32,36}... | collective-permute-start | bytes 98312 | tf_op jit(solution)/shard_map/ppermute | solution.py:17
  19.2 4.1 copy-start.2
  19.9 11.3 %collective-permute-start.2 = (bf16[128,1024]{0,1:T(8,128)(2,1)S(1)}, bf16[128,1024]{0,1:T(8,128)(2,1)S(1)}, u32[]{:S(2)}, u32[]{:S(2)}) collective-permute-start(bf16[128,1024]{0,1:T(8,128)(2,1)S(1)} %bitcast.60), channel_id=1, source_target_pairs={{0,1},{1,2},{2,3},{3,0},{4,5},{5,6},{6,7},{7,4},{8,9},{9,10},{10,1... | collective-permute-start | bytes 786440 | tf_op jit(solution)/shard_map/ppermute | solution.py:69
  31.3 10.5 %collective-permute-start.3 = (bf16[128,1024]{0,1:T(8,128)(2,1)S(1)}, bf16[128,1024]{0,1:T(8,128)(2,1)S(1)}, u32[]{:S(2)}, u32[]{:S(2)}) collective-permute-start(bf16[128,1024]{0,1:T(8,128)(2,1)S(1)} %collective-permute-done.2), channel_id=1, source_target_pairs={{0,1},{1,2},{2,3},{3,0},{4,5},{5,6},{6,7},{7,4},{8,9},{9,10},{10,1... | collective-permute-start | bytes 786440 | tf_op jit(solution)/shard_map/ppermute | solution.py:69
  41.7 9.5 %collective-permute-start.4 = (bf16[128,1024]{0,1:T(8,128)(2,1)S(1)}, bf16[128,1024]{0,1:T(8,128)(2,1)S(1)}, u32[]{:S(2)}, u32[]{:S(2)}) collective-permute-start(bf16[128,1024]{0,1:T(8,128)(2,1)S(1)} %collective-permute-done.3), channel_id=1, source_target_pairs={{0,1},{1,2},{2,3},{3,0},{4,5},{5,6},{6,7},{7,4},{8,9},{9,10},{10,1... | collective-permute-start | bytes 786440 | tf_op jit(solution)/shard_map/ppermute | solution.py:69
  44.3 55.1 %copy-start.1 = (bf16[128,720]{0,1:T(8,128)(2,1)S(1)}, bf16[128,720]{0,1:T(8,128)(2,1)}, u32[]{:S(2)}) copy-start(bf16[128,720]{0,1:T(8,128)(2,1)} %param.18) | copy-start | bytes 552964
  57.1 58.0 %copy-start.3 = (f32[720]{0:T(1024)S(1)}, f32[720]{0:T(1024)}, u32[]{:S(2)}) copy-start(f32[720]{0:T(1024)} %param.20) | copy-start | bytes 8644
  212.4 3.0 copy-start.5
  264.7 6.6 %collective-permute-start.5 = (bf16[1280,12]{0,1:T(8,128)(2,1)S(1)}, bf16[1280,12]{0,1:T(8,128)(2,1)S(1)}, u32[]{:S(2)}, u32[]{:S(2)}) collective-permute-start(bf16[1280,12]{0,1:T(8,128)(2,1)S(1)} %slice.10), channel_id=1, source_target_pairs={{0,1},{1,2},{2,3},{4,5},{5,6},{6,7},{8,9},{9,10},{10,11},{12,13},{... | collective-permute-start | bytes 92168
  266.0 5.9 %collective-permute-start.6 = (bf16[1280,12]{0,1:T(8,128)(2,1)S(1)}, bf16[1280,12]{0,1:T(8,128)(2,1)S(1)}, u32[]{:S(2)}, u32[]{:S(2)}) collective-permute-start(bf16[1280,12]{0,1:T(8,128)(2,1)S(1)} %slice.11), channel_id=1, source_target_pairs={{0,1},{1,2},{2,3},{4,5},{5,6},{6,7},{8,9},{9,10},{10,11},{12,13},{... | collective-permute-start | bytes 92168
  313.9 14.5 %copy-start.4 = (bf16[128,4]{0,1:T(4,128)(2,1)S(1)}, bf16[128,4]{0,1:T(4,128)(2,1)}, u32[]{:S(2)}) copy-start(bf16[128,4]{0,1:T(4,128)(2,1)} %param.22) | copy-start | bytes 3076
  313.9 89.5 %all-to-all-start.1 = ((bf16[128,10,720]{2,1,0:T(8,128)(2,1)}), bf16[128,10,720]{2,1,0:T(8,128)(2,1)}, u32[]{:S(2)}, u32[]{:S(2)}) async-start(bf16[128,10,720]{2,1,0:T(8,128)(2,1)} %reshape.192), calls=%async_computation.1 | async-start | bytes 6291456 | tf_op jit(solution)/shard_map/all_to_all | solution.py:121
Sparse Core Ops, SparseCore 0:
  10.5 88.8 all-gather.3
  273.9 28.9 all-gather.5
